TPU v7x, 256 devices: a whole 4x4x8 slice. The times are simulated.
256 devices in a mesh: tok: 16 (over y, x), col: 16 (over z, core).
Axes of the slice: x: 4, y: 4, z: 8, core: 2. Of those that a mesh axis runs over, the one named last changes fastest.
Arguments:
- activations: bfloat16 [32768, 8192], P('tok', 'col'), may hold values from -60 to 60, as said below
- weight: bfloat16 [8192, 8192], P('tok', 'col'), may hold values from -6 to 6
- keep_mask: int32 [8192, 8192], P('tok', 'col'), may hold values from 0 to 1
Outputs:
- new_weight: bfloat16 [8192, 8192], P('tok', 'col')
Inputs may be any that keep to these rules, and one draw needn't show every extreme that they name: activations of calibration tokens.
All inputs are finite; a program needn't handle non-finite values.
Results may differ from a plain program's by a relative error of at most 0.00115.
Values may be sent and summed in bfloat16 or wider, within the bound.
A program may use at most 64 MiB of HBM per device.

v0:
```python
import jax
import jax.numpy as jnp
from jax import lax
from jax.sharding import PartitionSpec as P

B = 1024
ITERS = 4


def split(x):
    high = lax.reduce_precision(x, exponent_bits=8, mantissa_bits=7)
    return (high.astype(jnp.bfloat16), (x - high).astype(jnp.bfloat16))


def mm(a, b, dims=(((1,), (0,)), ((), ()))):
    return lax.dot_general(a, b, dims, preferred_element_type=jnp.float32)


def per_device(activations, weight, keep_mask):
    n_col = lax.axis_size("col")
    n_tok = lax.axis_size("tok")
    tok_rows = activations.shape[0]
    panel_width = B // n_col
    total_count = tok_rows * n_tok
    pruned = jnp.where(
        keep_mask[:, :panel_width] == 0, weight[:, :panel_width], jnp.zeros((), jnp.bfloat16)
    )
    panel = lax.all_gather(activations[:, :panel_width], "col", axis=1, tiled=True)
    partial_panel = mm(activations, panel, (((0,), (0,)), ((), ())))
    pruned_panel = lax.all_gather(pruned, "col", axis=1, tiled=True)
    hessian_panel = lax.psum(partial_panel, "tok") / total_count
    block = lax.all_gather(hessian_panel[:panel_width], "col", axis=0, tiled=True)
    rows = lax.broadcasted_iota(jnp.int32, (B, B), 0)
    columns = lax.broadcasted_iota(jnp.int32, (B, B), 1)
    on_diagonal = rows == columns
    mean_diagonal = jnp.sum(jnp.where(on_diagonal, block, 0.0)) / B
    damped = block + jnp.where(on_diagonal, 0.01 * mean_diagonal, 0.0)
    scale = lax.rsqrt(jnp.sum(damped * damped))
    g = damped * scale
    y = pruned_panel.astype(jnp.float32)
    for sweep in range(ITERS):
        g_high = g.astype(jnp.bfloat16)
        y_high, y_low = split(y)
        y = 2.0 * y - (mm(y_high, g_high) + mm(y_low, g_high))
        if sweep < ITERS - 1:
            g = 2.0 * g - mm(g_high, g_high)
    y_high, y_low = split(y * scale)
    h_high, h_low = split(hessian_panel)
    nt = (((1,), (1,)), ((), ()))
    correction = mm(y_high, h_high, nt) + mm(y_low, h_high, nt) + mm(y_high, h_low, nt)
    kept = keep_mask.astype(jnp.float32)
    return (kept * (weight.astype(jnp.float32) - correction)).astype(jnp.bfloat16)


def solution(mesh):
    return jax.shard_map(
        per_device,
        mesh=mesh,
        in_specs=(P("tok", "col"), P("tok", "col"), P("tok", "col")),
        out_specs=P("tok", "col"),
        check_vma=False,
    )
```

profile of v0, /device:TPU:1, one launch (start us, length us, event | category | flops | bytes accessed | tf_op | source)
XLA Modules:
  0.0 284.6 jit_solution(3406045359667828655)
XLA Ops:
  6.5 0.0 all-gather.6.cloned.1.call-start
  6.5 1.2 slice.14
  7.8 0.9 copy.10
  8.7 0.0 all-gather.6.cloned.1.call-update
  8.7 0.0 all-reduce.2.cloned.1.call-start
  8.7 46.8 %all-gather.6.cloned.1.call-done = bf16[2048,1024]{0,1:T(8,128)(2,1)} async-done(((bf16[2048,64]{0,1:T(8,128)(2,1)}), bf16[2048,1024]{0,1:T(8,128)(2,1)}) %all-gather.6.cloned.1.call-update) | async-done | bytes 4194320 | tf_op jit(solution)/shard_map/all_gather | solution.py:28
  55.5 0.0 copy-done.4
  55.6 5.9 %fusion.29 = f32[512,1024]{1,0:T(8,128)} fusion(bf16[2048,512]{1,0:T(8,128)(2,1)S(1)} %copy-done.4, bf16[2048,1024]{0,1:T(8,128)(2,1)} %all-gather.6.cloned.1.call-done), kind=kOutput, calls=%fused_computation.50 | convolution fusion | flops 2147483648 | bytes 8388608 | tf_op jit(solution)/shard_map/dot_general | solution.py:16
  61.5 0.0 all-reduce.2.cloned.1.call-update
  61.5 0.0 all-gather.4.cloned.1.call-start
  61.5 0.8 slice-done.1
  62.4 0.1 copy.9
  62.5 0.0 slice-done
  62.5 0.1 copy.8
  62.6 0.6 compare_select_fusion
  63.2 0.0 all-gather.4.cloned.1.call-update
  63.3 0.0 all-gather.8.cloned.1.call-start
  63.3 95.8 %all-reduce.2.cloned.1.call-done = f32[512,1024]{1,0:T(8,128)} async-done(((f32[512,1024]{1,0:T(8,128)}), f32[512,1024]{1,0:T(8,128)}) %all-reduce.2.cloned.1.call-update) | async-done | bytes 2097168 | tf_op jit(solution)/shard_map/psum | solution.py:31
  159.1 1.8 broadcast_multiply_fusion
  160.9 0.7 slice.16
  161.6 0.0 all-gather.8.cloned.1.call-update
  161.6 39.0 %all-gather.4.cloned.1.call-done = bf16[512,1024]{0,1:T(8,128)(2,1)} async-done(((bf16[512,64]{0,1:T(8,128)(2,1)}), bf16[512,1024]{0,1:T(8,128)(2,1)}) %all-gather.4.cloned.1.call-update) | async-done | bytes 1048592 | tf_op jit(solution)/shard_map/all_gather | solution.py:30
  200.6 1.7 copy.6
  202.3 41.0 %all-gather.8.cloned.1.call-done = f32[1024,1024]{1,0:T(8,128)} async-done(((f32[64,1024]{1,0:T(8,128)}), f32[1024,1024]{1,0:T(8,128)}) %all-gather.8.cloned.1.call-update) | async-done | bytes 4194320 | tf_op jit(solution)/shard_map/all_gather | solution.py:32
  243.3 2.9 %select_reduce_fusion = f32[]{:T(128)} fusion(f32[1024,1024]{1,0:T(8,128)} %all-gather.8.cloned.1.call-done), kind=kLoop, calls=%fused_computation.5 | loop fusion | flops 3145727 | bytes 4194308 | tf_op jit(solution)/shard_map/reduce_sum | solution.py:36
  246.9 3.9 %multiply_reduce_fusion = f32[]{:T(128)} fusion(f32[1024,1024]{1,0:T(8,128)} %all-gather.8.cloned.1.call-done, f32[]{:T(128)S(6)} %mul_shard_map.3), kind=kLoop, calls=%fused_computation.3 | loop fusion | flops 5242879 | bytes 4194312 | tf_op jit(solution)/shard_map/reduce_sum | solution.py:38
  251.4 7.0 %multiply_subtract_fusion.1 = f32[1024,1024]{1,0:T(8,128)S(1)} fusion(f32[1024,1024]{1,0:T(8,128)} %all-gather.8.cloned.1.call-done, f32[]{:T(128)S(6)} %rsqrt.3, f32[]{:T(128)S(6)} %mul_shard_map.3), kind=kOutput, calls=%fused_computation.2 | convolution fusion | flops 2159017984 | bytes 8388616 | tf_op jit(solution)/shard_map/dot_general | solution.py:16
  258.5 0.0 copy-start.1
  258.5 2.3 multiply_subtract_fusion
  260.8 0.0 copy-done.1
  260.8 1.3 fusion.20
  262.1 1.4 fusion.6
  263.5 1.3 fusion.17
  264.8 1.3 add_subtract_fusion.1
  266.2 2.4 subtract_convert_fusion
  268.5 1.3 fusion.18
  269.8 1.6 add_subtract_fusion
  271.5 1.3 fusion.19
  272.7 0.0 copy-start
  272.7 1.4 subtract_multiply_fusion
  274.1 0.2 copy-done
  274.3 0.7 fusion.22
  275.1 0.0 copy-start.2
  275.1 0.0 copy-start.3
  275.1 0.7 convolution_add_fusion.1
  275.9 0.4 copy-done.2
  276.3 0.1 copy-done.3
  276.4 1.6 fusion.10
  (3 shorter events, 0.0 us)
Async XLA Ops:
  6.5 49.0 %copy-start.4 = (bf16[2048,512]{1,0:T(8,128)(2,1)S(1)}, bf16[2048,512]{1,0:T(8,128)(2,1)}, u32[]{:S(2)}) copy-start(bf16[2048,512]{1,0:T(8,128)(2,1)} %param.3) | copy-start | bytes 6291460
  6.5 49.0 %all-gather.6.cloned.1.call-start = ((), (), s32[]{:S(2)}) async-start(), calls=%async_computation.1 | async-start | bytes 4456448 | tf_op jit(solution)/shard_map/all_gather | solution.py:28
  8.7 150.4 %all-reduce.2.cloned.1.call-start = ((), (), s32[]{:S(2)}) async-start(), calls=%async_computation.2 | async-start | bytes 4194304 | tf_op jit(solution)/shard_map/psum | solution.py:31
  61.5 0.9 slice-start.1
  61.5 1.0 slice-start
  61.5 139.1 %all-gather.4.cloned.1.call-start = ((), (), s32[]{:S(2)}) async-start(), calls=%async_computation | async-start | bytes 1114112 | tf_op jit(solution)/shard_map/all_gather | solution.py:30
  63.3 180.0 %all-gather.8.cloned.1.call-start = ((), (), s32[]{:S(2)}) async-start(), calls=%async_computation.3 | async-start | bytes 4456448 | tf_op jit(solution)/shard_map/all_gather | solution.py:32
  258.5 2.4 copy-start.1
  272.7 1.6 copy-start
  275.1 1.2 copy-start.2
  275.1 1.3 copy-start.3
Sparse Core Ops, SparseCore 0:
  9.2 46.3 all-gather.5
  61.6 97.4 all-reduce.1
  161.1 39.5 all-gather.3
  202.4 40.7 all-gather.7
where the time goes:
time: 285 us
  waiting for transfers between devices  223 us (78%)
  matrix products  31.6 us (11%)
  between operations  14.6 us (5%)
  other arithmetic  9.21 us (3%)
  local copies, waits for them, and re-layouts  6.38 us (2%)
    psum x1, waiting for transfers between devices, per_device(): hessian_panel = lax.psum(partial_panel, 'tok') / total_count  95.8 us
    all_gather x1, waiting for transfers between devices, per_device(): lax.all_gather(activations[:, :panel_width], 'col', axis=1, tiled=True)  46.8 us
    all_gather x1, waiting for transfers between devices, per_device(): lax.all_gather(hessian_panel[:panel_width], 'col', axis=0, tiled=True)  41 us
    all_gather x1, waiting for transfers between devices, per_device(): pruned_panel = lax.all_gather(pruned, 'col', axis=1, tiled=True)  39 us
    dot_general x15, matrix products, mm(): return lax.dot_general(a, b, dims, preferred_element_type=jnp.float32)  31.6 us
  transfers between devices with their start and end apart: 4, of which 4 were waited for; matrix products, arithmetic and copies ran while one was open for 2% of the time, Pallas kernels for 0%

commit v1 on v0

--- a/solution.py
+++ b/solution.py
@@ -28,7 +28,7 @@
     panel = lax.all_gather(activations[:, :panel_width], "col", axis=1, tiled=True)
     partial_panel = mm(activations, panel, (((0,), (0,)), ((), ())))
     pruned_panel = lax.all_gather(pruned, "col", axis=1, tiled=True)
-    hessian_panel = lax.psum(partial_panel, "tok") / total_count
+    hessian_panel = jnp.sum(lax.all_gather(partial_panel, "tok"), 0) / total_count
     block = lax.all_gather(hessian_panel[:panel_width], "col", axis=0, tiled=True)
     rows = lax.broadcasted_iota(jnp.int32, (B, B), 0)
     columns = lax.broadcasted_iota(jnp.int32, (B, B), 1)

time: 285 us -> 387 us (1.36)
  waiting for transfers between devices: 223 us -> 314 us
  other arithmetic: 9.21 us -> 19.8 us
    all_gather x0 -> x1, waiting for transfers between devices: none -> 199 us  [per_device(): lax.all_gather(partial_panel, 'tok')]
    psum x1 -> x0, waiting for transfers between devices: 95.8 us -> none  [per_device(): hessian_panel = lax.psum(partial_panel, 'tok') / total_count]
    reduce_sum x0 -> x1, other arithmetic: none -> 12.1 us  [per_device(): jnp.sum(lax.all_gather(partial_panel, 'tok'), 0) / total_count]
    all_gather x1, waiting for transfers between devices: 39 us -> 27.6 us  [per_device(): pruned_panel = lax.all_gather(pruned, 'col', axis=1, tiled=True)]
  transfers between devices with their start and end apart: 4 -> 4, of which waited for: 4 -> 4; matrix products, arithmetic and copies ran while one was open for 2% -> 4% of each run, Pallas kernels for 0% -> 0%
where the time goes in v1:
time: 387 us; the launch traced here: 386 us
  waiting for transfers between devices  314 us (81%)
  matrix products  31.8 us (8%)
  other arithmetic  19.8 us (5%)
  between operations  14.6 us (4%)
  local copies, waits for them, and re-layouts  6.14 us (2%)
    all_gather x1, waiting for transfers between devices, per_device(): lax.all_gather(partial_panel, 'tok')  199 us
    all_gather x1, waiting for transfers between devices, per_device(): lax.all_gather(activations[:, :panel_width], 'col', axis=1, tiled=True)  46.8 us
    all_gather x1, waiting for transfers between devices, per_device(): lax.all_gather(hessian_panel[:panel_width], 'col', axis=0, tiled=True)  40.8 us
    dot_general x15, matrix products, mm(): return lax.dot_general(a, b, dims, preferred_element_type=jnp.float32)  31.8 us
    all_gather x1, waiting for transfers between devices, per_device(): pruned_panel = lax.all_gather(pruned, 'col', axis=1, tiled=True)  27.6 us
    reduce_sum x1, other arithmetic, per_device(): jnp.sum(lax.all_gather(partial_panel, 'tok'), 0) / total_count  12.1 us
  transfers between devices with their start and end apart: 4, of which 4 were waited for; matrix products, arithmetic and copies ran while one was open for 4% of the time, Pallas kernels for 0%

profile of v1, /device:TPU:1, one launch (start us, length us, event | category | flops | bytes accessed | tf_op | source)
XLA Modules:
  0.0 386.3 jit_solution(1877371268922955380)
XLA Ops:
  6.5 0.0 copy-start.3
  6.5 0.0 all-gather.8.cloned.1.call-start
  6.5 1.2 slice.14
  7.8 0.9 copy.10
  8.7 0.0 all-gather.8.cloned.1.call-update
  8.7 0.0 all-gather.12.cloned.1.call-start
  8.7 46.8 %all-gather.8.cloned.1.call-done = bf16[2048,1024]{0,1:T(8,128)(2,1)} async-done(((bf16[2048,64]{0,1:T(8,128)(2,1)}), bf16[2048,1024]{0,1:T(8,128)(2,1)}) %all-gather.8.cloned.1.call-update) | async-done | bytes 4194320 | tf_op jit(solution)/shard_map/all_gather | solution.py:28
  55.5 0.0 copy-done.3
  55.6 5.9 %fusion.29 = f32[512,1024]{1,0:T(8,128)} fusion(bf16[2048,512]{1,0:T(8,128)(2,1)S(1)} %copy-done.3, bf16[2048,1024]{0,1:T(8,128)(2,1)} %all-gather.8.cloned.1.call-done), kind=kOutput, calls=%fused_computation.50 | convolution fusion | flops 2147483648 | bytes 8388608 | tf_op jit(solution)/shard_map/dot_general | solution.py:16
  61.5 0.0 all-gather.12.cloned.1.call-update
  61.5 0.0 all-gather.6.cloned.1.call-start
  61.5 0.9 slice-done
  62.4 0.1 copy.8
  62.5 0.0 slice-done.1
  62.5 0.1 copy.9
  62.6 0.6 compare_select_fusion
  63.3 0.0 all-gather.6.cloned.1.call-update
  63.3 0.0 all-gather.10.cloned.1.call-start
  63.3 198.5 %all-gather.12.cloned.1.call-done = f32[8192,1024]{1,0:T(8,128)} async-done(((f32[512,1024]{1,0:T(8,128)}), f32[8192,1024]{1,0:T(8,128)}) %all-gather.12.cloned.1.call-update) | async-done | bytes 33554448 | tf_op jit(solution)/shard_map/all_gather | solution.py:31
  261.9 12.1 %reduce_sum.27 = f32[512,1024]{1,0:T(8,128)S(1)} reduce(f32[16,512,1024]{2,1,0:T(8,128)} %bitcast.5, f32[]{:T(128)} %constant.4.clone.1), dimensions={0}, to_apply=%region_0.1 | reduce | flops 7864320 | bytes 35651588 | tf_op jit(solution)/shard_map/reduce_sum | solution.py:31
  274.0 0.2 broadcast_multiply_fusion
  274.2 0.7 slice.16
  274.9 0.0 all-gather.10.cloned.1.call-update
  275.0 27.6 %all-gather.6.cloned.1.call-done = bf16[512,1024]{0,1:T(8,128)(2,1)} async-done(((bf16[512,64]{0,1:T(8,128)(2,1)}), bf16[512,1024]{0,1:T(8,128)(2,1)}) %all-gather.6.cloned.1.call-update) | async-done | bytes 1048592 | tf_op jit(solution)/shard_map/all_gather | solution.py:30
  302.5 1.7 copy.6
  304.2 40.8 %all-gather.10.cloned.1.call-done = f32[1024,1024]{1,0:T(8,128)} async-done(((f32[64,1024]{1,0:T(8,128)}), f32[1024,1024]{1,0:T(8,128)}) %all-gather.10.cloned.1.call-update) | async-done | bytes 4194320 | tf_op jit(solution)/shard_map/all_gather | solution.py:32
  345.0 2.9 select_reduce_fusion
  348.6 3.9 %multiply_reduce_fusion = f32[]{:T(128)} fusion(f32[1024,1024]{1,0:T(8,128)} %all-gather.10.cloned.1.call-done, f32[]{:T(128)S(6)} %mul_shard_map.3), kind=kLoop, calls=%fused_computation.3 | loop fusion | flops 5242879 | bytes 4194312 | tf_op jit(solution)/shard_map/reduce_sum | solution.py:38
  353.2 7.1 %multiply_subtract_fusion.1 = f32[1024,1024]{1,0:T(8,128)S(1)} fusion(f32[1024,1024]{1,0:T(8,128)} %all-gather.10.cloned.1.call-done, f32[]{:T(128)S(6)} %rsqrt.3, f32[]{:T(128)S(6)} %mul_shard_map.3), kind=kOutput, calls=%fused_computation.2 | convolution fusion | flops 2159017984 | bytes 8388616 | tf_op jit(solution)/shard_map/dot_general | solution.py:16
  360.3 0.0 copy-start
  360.3 2.3 multiply_subtract_fusion
  362.6 0.0 copy-done
  362.6 1.3 fusion.20
  364.0 1.4 fusion.6
  365.3 1.3 fusion.17
  366.6 1.3 add_subtract_fusion.1
  368.0 2.4 subtract_convert_fusion
  370.3 1.3 fusion.18
  371.6 1.6 add_subtract_fusion
  373.3 1.3 fusion.19
  374.5 1.4 subtract_multiply_fusion
  376.0 0.8 fusion.22
  376.7 0.0 copy-start.1
  376.7 0.0 copy-start.2
  376.8 0.8 convolution_add_fusion.1
  377.6 0.4 copy-done.1
  378.0 0.1 copy-done.2
  378.1 1.6 fusion.10
  (2 shorter events, 0.0 us)
Async XLA Ops:
  6.5 49.0 %copy-start.3 = (bf16[2048,512]{1,0:T(8,128)(2,1)S(1)}, bf16[2048,512]{1,0:T(8,128)(2,1)}, u32[]{:S(2)}) copy-start(bf16[2048,512]{1,0:T(8,128)(2,1)} %param.3) | copy-start | bytes 6291460
  6.5 49.0 %all-gather.8.cloned.1.call-start = ((), (), s32[]{:S(2)}) async-start(), calls=%async_computation.1 | async-start | bytes 4456448 | tf_op jit(solution)/shard_map/all_gather | solution.py:28
  8.7 253.2 %all-gather.12.cloned.1.call-start = ((), (), s32[]{:S(2)}) async-start(), calls=%async_computation.3 | async-start | bytes 35651584 | tf_op jit(solution)/shard_map/all_gather | solution.py:31
  61.5 0.9 slice-start
  61.5 1.1 slice-start.1
  61.5 241.0 %all-gather.6.cloned.1.call-start = ((), (), s32[]{:S(2)}) async-start(), calls=%async_computation | async-start | bytes 1114112 | tf_op jit(solution)/shard_map/all_gather | solution.py:30
  63.3 281.7 %all-gather.10.cloned.1.call-start = ((), (), s32[]{:S(2)}) async-start(), calls=%async_computation.2 | async-start | bytes 4456448 | tf_op jit(solution)/shard_map/all_gather | solution.py:32
  360.3 2.4 copy-start
  376.7 1.2 copy-start.1
  376.7 1.3 copy-start.2
Sparse Core Ops, SparseCore 0:
  9.2 46.3 all-gather.7
  61.6 200.2 all-gather.11
  263.7 38.7 all-gather.5
  304.2 40.7 all-gather.9
